TPU v7x, 32 devices: a whole 2x2x4 slice. The times are simulated.
32 devices in a mesh: col: 8 (over y, x, core), row: 4 (over z).
Axes of the slice: x: 2, y: 2, z: 4, core: 2. Of those that a mesh axis runs over, the one named last changes fastest.
Arguments:
- matrix: float32 [16, 512, 4096], P(None, 'row', 'col'), may hold values from -0.4 to 2.4, as said below
- pivots: int32 [8, 512], replicated, may hold values from 0 to 511, as said below
- seeds: float32 [8, 512, 512], P('col'), may hold values from -1 to 2, as said below
Outputs:
- factors: float32 [16, 512, 4096], P(None, 'row', 'col')
Inputs may be any that keep to these rules, and one draw needn't show every extreme that they name: Each row of pivots is an ordering of 0 .. 511. Block (r, j) of matrix is zero where r and j differ by more than 8. seeds[k] approximates the inverse of block (k, k) of matrix after the replacement of rows by pivots[k].
All inputs are finite; a program needn't handle non-finite values.
Results may differ from a plain program's by a relative error of at most 0.0001.
Values sent between devices are 32-bit elements; how exact they have to be, the bound alone decides.
A program may use at most 64 MiB of HBM per device.

v0:
```python
import jax
import jax.numpy as jnp
from jax import lax
from jax.sharding import PartitionSpec as P

HB = 8
SWEEPS = 2


def from_root(block, axis, source):
    block = jnp.where(lax.axis_index(axis) == source, block, jnp.zeros_like(block))
    return lax.psum(block, axis)


def dot_high(left, right):
    return jnp.dot(left, right, precision=lax.Precision.HIGHEST, preferred_element_type=jnp.float32)


def refine(pivot_block, approx, identity):
    for sweep_index in range(SWEEPS):
        approx = dot_high(approx, 2.0 * identity - dot_high(pivot_block, approx))
    return approx


def local(matrix, pivots, seeds):
    col_count = lax.axis_size("col")
    col_index = lax.axis_index("col")
    row_index = lax.axis_index("row")
    row_share = matrix.shape[1]
    panel_width = matrix.shape[2]
    identity = jnp.eye(panel_width, dtype=jnp.float32)
    seed_block = seeds[0]

    def eliminate(panel_index, factors):
        local_row = lax.dynamic_index_in_dim(factors, panel_index, 0, keepdims=False)
        block_row = lax.all_gather(local_row, "row", axis=0, tiled=True)
        ordering = lax.dynamic_index_in_dim(pivots, panel_index, 0, keepdims=False)
        swapped = jnp.take(block_row, ordering, axis=0)
        block_row = jnp.where(col_index >= panel_index, swapped, block_row)
        local_row = lax.dynamic_slice_in_dim(block_row, row_index * row_share, row_share, 0)
        factors = lax.dynamic_update_index_in_dim(factors, local_row, panel_index, 0)
        is_owner = col_index == panel_index
        approx = lax.cond(
            is_owner, lambda: refine(block_row, seed_block, identity), lambda: seed_block
        )
        below_rows = lax.dynamic_slice_in_dim(factors, panel_index + 1, HB, 0)
        below_flat = below_rows.reshape(HB * row_share, panel_width)
        scaled = lax.cond(is_owner, lambda: dot_high(below_flat, approx), lambda: below_flat)
        in_reach = (col_index > panel_index) & (col_index <= panel_index + HB)
        arrived = from_root(scaled, "col", panel_index)
        updated = below_flat - dot_high(arrived, block_row)
        result = jnp.where(is_owner, scaled, jnp.where(in_reach, updated, below_flat))
        return lax.dynamic_update_slice_in_dim(
            factors, result.reshape(HB, row_share, panel_width), panel_index + 1, 0
        )

    return lax.fori_loop(0, col_count, eliminate, matrix)


def solution(mesh):
    return jax.shard_map(
        local,
        mesh=mesh,
        in_specs=(P(None, "row", "col"), P(), P("col", None, None)),
        out_specs=P(None, "row", "col"),
        check_vma=False,
    )
```

profile of v0, /device:TPU:0, one launch (start us, length us, event | category | flops | bytes accessed | tf_op | source)
XLA Modules:
  0.0 1028.8 jit_solution(17869282881997952237)
XLA Ops:
  11.4 1010.8 %while.17 = (s32[]{:T(128)}, f32[16,128,512]{2,1,0:T(8,128)}, s32[]{:T(128)}, s32[8,512]{1,0:T(8,128)}, s32[]{:T(128)}, /*index=5*/f32[512,512]{1,0:T(8,128)S(1)...) while((s32[]{:T(128)}, f32[16,128,512]{2,1,0:T(8,128)}, ...), condition=%wide.region_6.7_spmd.clone.clone, body=%wide.region_0.6_spmd.clone.clone.sunk | while | flops 12889626624 | bytes 111953976 | solution.py:57
  15.0 29.5 %all-gather.6.cloned.1.call-done = f32[1,512,512]{2,1,0:T(8,128)} async-done(((f32[1,128,512]{2,1,0:T(8,128)}), f32[1,512,512]{2,1,0:T(8,128)}) %all-gather.6.cloned.1.call-update) | async-done | bytes 1048592 | tf_op jit(solution)/shard_map/while/body/eval_jaxpr/all_gather | solution.py:36
  50.7 11.3 %conditional.8 = (f32[512,512]{1,0:T(8,128)}) conditional(s32[]{:T(128)} %convert_element_type.27, f32[512,512]{1,0:T(8,128)S(1)} %get-tuple-element.345, (f32[512,512]{1,0:T(8,128)}, f32[512,512]{1,0:T(8,128)}, f32[512,512]{1,0:T(8,128)S(1)}, f32[512,512]{1,0:T(8,128)S(1)}) %tuple.77), branch_computations={%region_1.1_spmd, %region_2.2_spmd} | conditional | flops 6443499520 | bytes 18874404 | solution.py:43
  63.9 6.0 conditional.9
  63.9 6.0 fusion.5
  73.1 59.5 %all-reduce.2.cloned.1.call-done = f32[1024,512]{1,0:T(8,128)} async-done(((f32[1024,512]{1,0:T(8,128)}), f32[1024,512]{1,0:T(8,128)}) %all-reduce.2.cloned.1.call-update) | async-done | bytes 2097168 | tf_op jit(solution)/shard_map/while/body/eval_jaxpr/psum | solution.py:12
  132.6 5.9 fusion.27
  144.4 25.8 %all-gather.6.cloned.1.call-done = f32[1,512,512]{2,1,0:T(8,128)} async-done(((f32[1,128,512]{2,1,0:T(8,128)}), f32[1,512,512]{2,1,0:T(8,128)}) %all-gather.6.cloned.1.call-update) | async-done | bytes 1048592 | tf_op jit(solution)/shard_map/while/body/eval_jaxpr/all_gather | solution.py:36
  182.2 75.3 %all-reduce.2.cloned.1.call-done = f32[1024,512]{1,0:T(8,128)} async-done(((f32[1024,512]{1,0:T(8,128)}), f32[1024,512]{1,0:T(8,128)}) %all-reduce.2.cloned.1.call-update) | async-done | bytes 2097168 | tf_op jit(solution)/shard_map/while/body/eval_jaxpr/psum | solution.py:12
  257.5 5.3 fusion.27
  268.7 25.5 %all-gather.6.cloned.1.call-done = f32[1,512,512]{2,1,0:T(8,128)} async-done(((f32[1,128,512]{2,1,0:T(8,128)}), f32[1,512,512]{2,1,0:T(8,128)}) %all-gather.6.cloned.1.call-update) | async-done | bytes 1048592 | tf_op jit(solution)/shard_map/while/body/eval_jaxpr/all_gather | solution.py:36
  306.2 76.9 %all-reduce.2.cloned.1.call-done = f32[1024,512]{1,0:T(8,128)} async-done(((f32[1024,512]{1,0:T(8,128)}), f32[1024,512]{1,0:T(8,128)}) %all-reduce.2.cloned.1.call-update) | async-done | bytes 2097168 | tf_op jit(solution)/shard_map/while/body/eval_jaxpr/psum | solution.py:12
  394.4 26.3 %all-gather.6.cloned.1.call-done = f32[1,512,512]{2,1,0:T(8,128)} async-done(((f32[1,128,512]{2,1,0:T(8,128)}), f32[1,512,512]{2,1,0:T(8,128)}) %all-gather.6.cloned.1.call-update) | async-done | bytes 1048592 | tf_op jit(solution)/shard_map/while/body/eval_jaxpr/all_gather | solution.py:36
  432.6 76.5 %all-reduce.2.cloned.1.call-done = f32[1024,512]{1,0:T(8,128)} async-done(((f32[1024,512]{1,0:T(8,128)}), f32[1024,512]{1,0:T(8,128)}) %all-reduce.2.cloned.1.call-update) | async-done | bytes 2097168 | tf_op jit(solution)/shard_map/while/body/eval_jaxpr/psum | solution.py:12
  520.3 25.8 %all-gather.6.cloned.1.call-done = f32[1,512,512]{2,1,0:T(8,128)} async-done(((f32[1,128,512]{2,1,0:T(8,128)}), f32[1,512,512]{2,1,0:T(8,128)}) %all-gather.6.cloned.1.call-update) | async-done | bytes 1048592 | tf_op jit(solution)/shard_map/while/body/eval_jaxpr/all_gather | solution.py:36
  558.2 76.9 %all-reduce.2.cloned.1.call-done = f32[1024,512]{1,0:T(8,128)} async-done(((f32[1024,512]{1,0:T(8,128)}), f32[1024,512]{1,0:T(8,128)}) %all-reduce.2.cloned.1.call-update) | async-done | bytes 2097168 | tf_op jit(solution)/shard_map/while/body/eval_jaxpr/psum | solution.py:12
  646.3 26.3 %all-gather.6.cloned.1.call-done = f32[1,512,512]{2,1,0:T(8,128)} async-done(((f32[1,128,512]{2,1,0:T(8,128)}), f32[1,512,512]{2,1,0:T(8,128)}) %all-gather.6.cloned.1.call-update) | async-done | bytes 1048592 | tf_op jit(solution)/shard_map/while/body/eval_jaxpr/all_gather | solution.py:36
  684.6 76.5 %all-reduce.2.cloned.1.call-done = f32[1024,512]{1,0:T(8,128)} async-done(((f32[1024,512]{1,0:T(8,128)}), f32[1024,512]{1,0:T(8,128)}) %all-reduce.2.cloned.1.call-update) | async-done | bytes 2097168 | tf_op jit(solution)/shard_map/while/body/eval_jaxpr/psum | solution.py:12
  761.0 5.3 fusion.27
  772.2 25.8 %all-gather.6.cloned.1.call-done = f32[1,512,512]{2,1,0:T(8,128)} async-done(((f32[1,128,512]{2,1,0:T(8,128)}), f32[1,512,512]{2,1,0:T(8,128)}) %all-gather.6.cloned.1.call-update) | async-done | bytes 1048592 | tf_op jit(solution)/shard_map/while/body/eval_jaxpr/all_gather | solution.py:36
  810.1 77.8 %all-reduce.2.cloned.1.call-done = f32[1024,512]{1,0:T(8,128)} async-done(((f32[1024,512]{1,0:T(8,128)}), f32[1024,512]{1,0:T(8,128)}) %all-reduce.2.cloned.1.call-update) | async-done | bytes 2097168 | tf_op jit(solution)/shard_map/while/body/eval_jaxpr/psum | solution.py:12
  899.1 26.2 %all-gather.6.cloned.1.call-done = f32[1,512,512]{2,1,0:T(8,128)} async-done(((f32[1,128,512]{2,1,0:T(8,128)}), f32[1,512,512]{2,1,0:T(8,128)}) %all-gather.6.cloned.1.call-update) | async-done | bytes 1048592 | tf_op jit(solution)/shard_map/while/body/eval_jaxpr/all_gather | solution.py:36
  937.3 77.4 %all-reduce.2.cloned.1.call-done = f32[1024,512]{1,0:T(8,128)} async-done(((f32[1024,512]{1,0:T(8,128)}), f32[1024,512]{1,0:T(8,128)}) %all-reduce.2.cloned.1.call-update) | async-done | bytes 2097168 | tf_op jit(solution)/shard_map/while/body/eval_jaxpr/psum | solution.py:12
  1014.7 5.3 fusion.27
  (225 shorter events, 195.4 us)
Async XLA Ops:
  11.4 33.1 %all-gather.6.cloned.1.call-start = ((), (), s32[]{:S(2)}) async-start(), calls=%async_computation | async-start | bytes 1310720 | tf_op jit(solution)/shard_map/while/body/eval_jaxpr/all_gather | solution.py:36
  13.1 119.4 %all-reduce.2.cloned.1.call-start = ((), (), s32[]{:S(2)}) async-start(), calls=%async_computation.1 | async-start | bytes 4194304 | tf_op jit(solution)/shard_map/while/body/eval_jaxpr/psum | solution.py:12
  132.6 5.9 copy-start.4
  140.8 29.4 %all-gather.6.cloned.1.call-start = ((), (), s32[]{:S(2)}) async-start(), calls=%async_computation | async-start | bytes 1310720 | tf_op jit(solution)/shard_map/while/body/eval_jaxpr/all_gather | solution.py:36
  142.5 115.0 %all-reduce.2.cloned.1.call-start = ((), (), s32[]{:S(2)}) async-start(), calls=%async_computation.1 | async-start | bytes 4194304 | tf_op jit(solution)/shard_map/while/body/eval_jaxpr/psum | solution.py:12
  257.5 5.3 copy-start.4
  265.1 29.1 %all-gather.6.cloned.1.call-start = ((), (), s32[]{:S(2)}) async-start(), calls=%async_computation | async-start | bytes 1310720 | tf_op jit(solution)/shard_map/while/body/eval_jaxpr/all_gather | solution.py:36
  266.8 116.4 %all-reduce.2.cloned.1.call-start = ((), (), s32[]{:S(2)}) async-start(), calls=%async_computation.1 | async-start | bytes 4194304 | tf_op jit(solution)/shard_map/while/body/eval_jaxpr/psum | solution.py:12
  383.2 5.3 copy-start.4
  390.8 29.9 %all-gather.6.cloned.1.call-start = ((), (), s32[]{:S(2)}) async-start(), calls=%async_computation | async-start | bytes 1310720 | tf_op jit(solution)/shard_map/while/body/eval_jaxpr/all_gather | solution.py:36
  392.4 116.7 %all-reduce.2.cloned.1.call-start = ((), (), s32[]{:S(2)}) async-start(), calls=%async_computation.1 | async-start | bytes 4194304 | tf_op jit(solution)/shard_map/while/body/eval_jaxpr/psum | solution.py:12
  509.1 5.3 copy-start.4
  516.7 29.5 %all-gather.6.cloned.1.call-start = ((), (), s32[]{:S(2)}) async-start(), calls=%async_computation | async-start | bytes 1310720 | tf_op jit(solution)/shard_map/while/body/eval_jaxpr/all_gather | solution.py:36
  518.4 116.7 %all-reduce.2.cloned.1.call-start = ((), (), s32[]{:S(2)}) async-start(), calls=%async_computation.1 | async-start | bytes 4194304 | tf_op jit(solution)/shard_map/while/body/eval_jaxpr/psum | solution.py:12
  635.1 5.3 copy-start.4
  642.7 29.9 %all-gather.6.cloned.1.call-start = ((), (), s32[]{:S(2)}) async-start(), calls=%async_computation | async-start | bytes 1310720 | tf_op jit(solution)/shard_map/while/body/eval_jaxpr/all_gather | solution.py:36
  644.4 116.7 %all-reduce.2.cloned.1.call-start = ((), (), s32[]{:S(2)}) async-start(), calls=%async_computation.1 | async-start | bytes 4194304 | tf_op jit(solution)/shard_map/while/body/eval_jaxpr/psum | solution.py:12
  761.0 5.3 copy-start.4
  768.6 29.5 %all-gather.6.cloned.1.call-start = ((), (), s32[]{:S(2)}) async-start(), calls=%async_computation | async-start | bytes 1310720 | tf_op jit(solution)/shard_map/while/body/eval_jaxpr/all_gather | solution.py:36
  770.3 117.6 %all-reduce.2.cloned.1.call-start = ((), (), s32[]{:S(2)}) async-start(), calls=%async_computation.1 | async-start | bytes 4194304 | tf_op jit(solution)/shard_map/while/body/eval_jaxpr/psum | solution.py:12
  887.9 5.3 copy-start.4
  895.5 29.8 %all-gather.6.cloned.1.call-start = ((), (), s32[]{:S(2)}) async-start(), calls=%async_computation | async-start | bytes 1310720 | tf_op jit(solution)/shard_map/while/body/eval_jaxpr/all_gather | solution.py:36
  897.2 117.5 %all-reduce.2.cloned.1.call-start = ((), (), s32[]{:S(2)}) async-start(), calls=%async_computation.1 | async-start | bytes 4194304 | tf_op jit(solution)/shard_map/while/body/eval_jaxpr/psum | solution.py:12
  1014.7 5.3 copy-start.4
  (26 other events, 75.5 us)
Sparse Core Ops, SparseCore 0:
  13.8 30.6 all-gather.5
  73.2 59.3 all-reduce.1
  143.1 26.9 all-gather.5
  182.3 75.1 all-reduce.1
  267.1 27.0 all-gather.5
  306.3 76.7 all-reduce.1
  393.1 27.4 all-gather.5
  432.7 76.3 all-reduce.1
  519.1 27.0 all-gather.5
  558.3 76.7 all-reduce.1
  645.1 27.4 all-gather.5
  684.7 76.3 all-reduce.1
  771.0 27.0 all-gather.5
  810.2 77.6 all-reduce.1
  897.5 27.6 all-gather.5
  937.4 77.2 all-reduce.1
where the time goes:
time: 1030 us
  waiting for transfers between devices  808 us (78%)
  local copies, waits for them, and re-layouts  106 us (10%)
  matrix products  60 us (6%)
  other arithmetic  39.8 us (4%)
  between operations  13.1 us (1%)
    psum x8, waiting for transfers between devices, from_root(): return lax.psum(block, axis)  597 us
    all_gather x8, waiting for transfers between devices, eliminate(): block_row = lax.all_gather(local_row, 'row', axis=0, tiled=True)  211 us
    dot_general x13, matrix products, dot_high(): jnp.dot(left, right, precision=lax.Precision.HIGHEST, preferred_element_t...  60 us
    gather x8, local copies, waits for them, and re-layouts, eliminate(): swapped = jnp.take(block_row, ordering, axis=0)  32.5 us
  transfers between devices with their start and end apart: 16, of which 16 were waited for; matrix products, arithmetic and copies ran while one was open for 1% of the time, Pallas kernels for 0%

commit v1 on v0

--- a/solution.py
+++ b/solution.py
@@ -9,7 +9,7 @@
 
 def from_root(block, axis, source):
     block = jnp.where(lax.axis_index(axis) == source, block, jnp.zeros_like(block))
-    return lax.psum(block, axis)
+    return jnp.sum(lax.all_gather(block, axis), axis=0)
 
 
 def dot_high(left, right):

time: 1030 us -> 1340 us (1.30)
  waiting for transfers between devices: 808 us -> 1040 us
  other arithmetic: 39.8 us -> 115 us
    all_gather x0 -> x8, waiting for transfers between devices: none -> 820 us  [from_root(): return jnp.sum(lax.all_gather(block, axis), axis=0)]
    psum x8 -> x0, waiting for transfers between devices: 597 us -> none  [from_root(): return lax.psum(block, axis)]
    reduce_sum x0 -> x8, other arithmetic: none -> 75.3 us  [from_root(): return jnp.sum(lax.all_gather(block, axis), axis=0)]
where the time goes in v1:
time: 1340 us; the launch traced here: 1330 us
  waiting for transfers between devices  1040 us (78%)
  other arithmetic  115 us (9%)
  local copies, waits for them, and re-layouts  107 us (8%)
  matrix products  59 us (4%)
    all_gather x8, waiting for transfers between devices, from_root(): return jnp.sum(lax.all_gather(block, axis), axis=0)  820 us
    all_gather x8, waiting for transfers between devices, eliminate(): block_row = lax.all_gather(local_row, 'row', axis=0, tiled=True)  217 us
    reduce_sum x8, other arithmetic, from_root(): return jnp.sum(lax.all_gather(block, axis), axis=0)  75.3 us
    dot_general x13, matrix products, dot_high(): jnp.dot(left, right, precision=lax.Precision.HIGHEST, preferred_element_t...  59 us
    gather x8, local copies, waits for them, and re-layouts, eliminate(): swapped = jnp.take(block_row, ordering, axis=0)  32.4 us
  transfers between devices with their start and end apart: 16, of which 16 were waited for; matrix products, arithmetic and copies ran while one was open for 1% of the time, Pallas kernels for 0%

profile of v1, /device:TPU:0, one launch (start us, length us, event | category | flops | bytes accessed | tf_op | source)
XLA Modules:
  0.0 1333.9 jit_solution(7570783295702944159)
XLA Ops:
  11.4 1315.9 %while.17 = (s32[]{:T(128)}, f32[16,128,512]{2,1,0:T(8,128)}, s32[]{:T(128)}, s32[8,512]{1,0:T(8,128)}, s32[]{:T(128)}, /*index=5*/f32[512,512]{1,0:T(8,128)S(1)...) while((s32[]{:T(128)}, f32[16,128,512]{2,1,0:T(8,128)}, ...), condition=%wide.region_6.7_spmd.clone.clone, body=%wide.region_0.6_spmd.clone.clone.sunk | while | flops 12892772352 | bytes 179062912 | solution.py:57
  15.1 29.5 %all-gather.11.cloned.1.call-done = f32[1,512,512]{2,1,0:T(8,128)} async-done(((f32[1,128,512]{2,1,0:T(8,128)}), f32[1,512,512]{2,1,0:T(8,128)}) %all-gather.11.cloned.1.call-update) | async-done | bytes 1048592 | tf_op jit(solution)/shard_map/while/body/eval_jaxpr/all_gather | solution.py:36
  50.7 10.3 conditional.8
  73.1 87.4 %all-gather.13.cloned.1.call-done = f32[8192,512]{1,0:T(8,128)} async-done(((f32[1024,512]{1,0:T(8,128)}), f32[8192,512]{1,0:T(8,128)}) %all-gather.13.cloned.1.call-update) | async-done | bytes 16777232 | tf_op jit(solution)/shard_map/while/body/eval_jaxpr/all_gather | solution.py:12
  181.8 26.1 %all-gather.11.cloned.1.call-done = f32[1,512,512]{2,1,0:T(8,128)} async-done(((f32[1,128,512]{2,1,0:T(8,128)}), f32[1,512,512]{2,1,0:T(8,128)}) %all-gather.11.cloned.1.call-update) | async-done | bytes 1048592 | tf_op jit(solution)/shard_map/while/body/eval_jaxpr/all_gather | solution.py:36
  219.9 103.2 %all-gather.13.cloned.1.call-done = f32[8192,512]{1,0:T(8,128)} async-done(((f32[1024,512]{1,0:T(8,128)}), f32[8192,512]{1,0:T(8,128)}) %all-gather.13.cloned.1.call-update) | async-done | bytes 16777232 | tf_op jit(solution)/shard_map/while/body/eval_jaxpr/all_gather | solution.py:12
  323.2 9.4 reduce_sum.19
  343.8 26.4 %all-gather.11.cloned.1.call-done = f32[1,512,512]{2,1,0:T(8,128)} async-done(((f32[1,128,512]{2,1,0:T(8,128)}), f32[1,512,512]{2,1,0:T(8,128)}) %all-gather.11.cloned.1.call-update) | async-done | bytes 1048592 | tf_op jit(solution)/shard_map/while/body/eval_jaxpr/all_gather | solution.py:36
  382.3 104.8 %all-gather.13.cloned.1.call-done = f32[8192,512]{1,0:T(8,128)} async-done(((f32[1024,512]{1,0:T(8,128)}), f32[8192,512]{1,0:T(8,128)}) %all-gather.13.cloned.1.call-update) | async-done | bytes 16777232 | tf_op jit(solution)/shard_map/while/body/eval_jaxpr/all_gather | solution.py:12
  487.1 9.4 reduce_sum.19
  507.7 27.4 %all-gather.11.cloned.1.call-done = f32[1,512,512]{2,1,0:T(8,128)} async-done(((f32[1,128,512]{2,1,0:T(8,128)}), f32[1,512,512]{2,1,0:T(8,128)}) %all-gather.11.cloned.1.call-update) | async-done | bytes 1048592 | tf_op jit(solution)/shard_map/while/body/eval_jaxpr/all_gather | solution.py:36
  547.2 104.4 %all-gather.13.cloned.1.call-done = f32[8192,512]{1,0:T(8,128)} async-done(((f32[1024,512]{1,0:T(8,128)}), f32[8192,512]{1,0:T(8,128)}) %all-gather.13.cloned.1.call-update) | async-done | bytes 16777232 | tf_op jit(solution)/shard_map/while/body/eval_jaxpr/all_gather | solution.py:12
  651.6 9.4 reduce_sum.19
  672.2 27.3 %all-gather.11.cloned.1.call-done = f32[1,512,512]{2,1,0:T(8,128)} async-done(((f32[1,128,512]{2,1,0:T(8,128)}), f32[1,512,512]{2,1,0:T(8,128)}) %all-gather.11.cloned.1.call-update) | async-done | bytes 1048592 | tf_op jit(solution)/shard_map/while/body/eval_jaxpr/all_gather | solution.py:36
  711.5 104.8 %all-gather.13.cloned.1.call-done = f32[8192,512]{1,0:T(8,128)} async-done(((f32[1024,512]{1,0:T(8,128)}), f32[8192,512]{1,0:T(8,128)}) %all-gather.13.cloned.1.call-update) | async-done | bytes 16777232 | tf_op jit(solution)/shard_map/while/body/eval_jaxpr/all_gather | solution.py:12
  816.3 9.4 reduce_sum.19
  837.0 26.7 %all-gather.11.cloned.1.call-done = f32[1,512,512]{2,1,0:T(8,128)} async-done(((f32[1,128,512]{2,1,0:T(8,128)}), f32[1,512,512]{2,1,0:T(8,128)}) %all-gather.11.cloned.1.call-update) | async-done | bytes 1048592 | tf_op jit(solution)/shard_map/while/body/eval_jaxpr/all_gather | solution.py:36
  875.8 104.4 %all-gather.13.cloned.1.call-done = f32[8192,512]{1,0:T(8,128)} async-done(((f32[1024,512]{1,0:T(8,128)}), f32[8192,512]{1,0:T(8,128)}) %all-gather.13.cloned.1.call-update) | async-done | bytes 16777232 | tf_op jit(solution)/shard_map/while/body/eval_jaxpr/all_gather | solution.py:12
  980.2 9.4 reduce_sum.19
  1000.8 26.8 %all-gather.11.cloned.1.call-done = f32[1,512,512]{2,1,0:T(8,128)} async-done(((f32[1,128,512]{2,1,0:T(8,128)}), f32[1,512,512]{2,1,0:T(8,128)}) %all-gather.11.cloned.1.call-update) | async-done | bytes 1048592 | tf_op jit(solution)/shard_map/while/body/eval_jaxpr/all_gather | solution.py:36
  1039.6 105.7 %all-gather.13.cloned.1.call-done = f32[8192,512]{1,0:T(8,128)} async-done(((f32[1024,512]{1,0:T(8,128)}), f32[8192,512]{1,0:T(8,128)}) %all-gather.13.cloned.1.call-update) | async-done | bytes 16777232 | tf_op jit(solution)/shard_map/while/body/eval_jaxpr/all_gather | solution.py:12
  1145.3 9.4 reduce_sum.19
  1166.0 27.1 %all-gather.11.cloned.1.call-done = f32[1,512,512]{2,1,0:T(8,128)} async-done(((f32[1,128,512]{2,1,0:T(8,128)}), f32[1,512,512]{2,1,0:T(8,128)}) %all-gather.11.cloned.1.call-update) | async-done | bytes 1048592 | tf_op jit(solution)/shard_map/while/body/eval_jaxpr/all_gather | solution.py:36
  1205.1 105.3 %all-gather.13.cloned.1.call-done = f32[8192,512]{1,0:T(8,128)} async-done(((f32[1024,512]{1,0:T(8,128)}), f32[8192,512]{1,0:T(8,128)}) %all-gather.13.cloned.1.call-update) | async-done | bytes 16777232 | tf_op jit(solution)/shard_map/while/body/eval_jaxpr/all_gather | solution.py:12
  (249 shorter events, 241.8 us)
Async XLA Ops:
  11.4 33.1 %all-gather.11.cloned.1.call-start = ((), (), s32[]{:S(2)}) async-start(), calls=%async_computation | async-start | bytes 1310720 | tf_op jit(solution)/shard_map/while/body/eval_jaxpr/all_gather | solution.py:36
  13.1 147.3 %all-gather.13.cloned.1.call-start = ((), (), s32[]{:S(2)}) async-start(), calls=%async_computation.1 | async-start | bytes 18874368 | tf_op jit(solution)/shard_map/while/body/eval_jaxpr/all_gather | solution.py:12
  169.9 5.9 copy-start.5
  178.1 29.7 %all-gather.11.cloned.1.call-start = ((), (), s32[]{:S(2)}) async-start(), calls=%async_computation | async-start | bytes 1310720 | tf_op jit(solution)/shard_map/while/body/eval_jaxpr/all_gather | solution.py:36
  179.8 143.3 %all-gather.13.cloned.1.call-start = ((), (), s32[]{:S(2)}) async-start(), calls=%async_computation.1 | async-start | bytes 18874368 | tf_op jit(solution)/shard_map/while/body/eval_jaxpr/all_gather | solution.py:12
  332.6 5.3 copy-start.5
  340.2 30.1 %all-gather.11.cloned.1.call-start = ((), (), s32[]{:S(2)}) async-start(), calls=%async_computation | async-start | bytes 1310720 | tf_op jit(solution)/shard_map/while/body/eval_jaxpr/all_gather | solution.py:36
  341.9 145.2 %all-gather.13.cloned.1.call-start = ((), (), s32[]{:S(2)}) async-start(), calls=%async_computation.1 | async-start | bytes 18874368 | tf_op jit(solution)/shard_map/while/body/eval_jaxpr/all_gather | solution.py:12
  496.5 5.3 copy-start.5
  504.1 31.0 %all-gather.11.cloned.1.call-start = ((), (), s32[]{:S(2)}) async-start(), calls=%async_computation | async-start | bytes 1310720 | tf_op jit(solution)/shard_map/while/body/eval_jaxpr/all_gather | solution.py:36
  505.8 145.7 %all-gather.13.cloned.1.call-start = ((), (), s32[]{:S(2)}) async-start(), calls=%async_computation.1 | async-start | bytes 18874368 | tf_op jit(solution)/shard_map/while/body/eval_jaxpr/all_gather | solution.py:12
  661.0 5.3 copy-start.5
  668.6 30.9 %all-gather.11.cloned.1.call-start = ((), (), s32[]{:S(2)}) async-start(), calls=%async_computation | async-start | bytes 1310720 | tf_op jit(solution)/shard_map/while/body/eval_jaxpr/all_gather | solution.py:36
  670.3 146.1 %all-gather.13.cloned.1.call-start = ((), (), s32[]{:S(2)}) async-start(), calls=%async_computation.1 | async-start | bytes 18874368 | tf_op jit(solution)/shard_map/while/body/eval_jaxpr/all_gather | solution.py:12
  825.7 5.3 copy-start.5
  833.3 30.4 %all-gather.11.cloned.1.call-start = ((), (), s32[]{:S(2)}) async-start(), calls=%async_computation | async-start | bytes 1310720 | tf_op jit(solution)/shard_map/while/body/eval_jaxpr/all_gather | solution.py:36
  835.0 145.1 %all-gather.13.cloned.1.call-start = ((), (), s32[]{:S(2)}) async-start(), calls=%async_computation.1 | async-start | bytes 18874368 | tf_op jit(solution)/shard_map/while/body/eval_jaxpr/all_gather | solution.py:12
  989.6 5.3 copy-start.5
  997.1 30.4 %all-gather.11.cloned.1.call-start = ((), (), s32[]{:S(2)}) async-start(), calls=%async_computation | async-start | bytes 1310720 | tf_op jit(solution)/shard_map/while/body/eval_jaxpr/all_gather | solution.py:36
  998.9 146.5 %all-gather.13.cloned.1.call-start = ((), (), s32[]{:S(2)}) async-start(), calls=%async_computation.1 | async-start | bytes 18874368 | tf_op jit(solution)/shard_map/while/body/eval_jaxpr/all_gather | solution.py:12
  1154.7 5.3 copy-start.5
  1162.3 30.7 %all-gather.11.cloned.1.call-start = ((), (), s32[]{:S(2)}) async-start(), calls=%async_computation | async-start | bytes 1310720 | tf_op jit(solution)/shard_map/while/body/eval_jaxpr/all_gather | solution.py:36
  1164.0 146.3 %all-gather.13.cloned.1.call-start = ((), (), s32[]{:S(2)}) async-start(), calls=%async_computation.1 | async-start | bytes 18874368 | tf_op jit(solution)/shard_map/while/body/eval_jaxpr/all_gather | solution.py:12
  1319.8 5.3 copy-start.5
  (34 other events, 83.3 us)
Sparse Core Ops, SparseCore 0:
  13.8 30.6 all-gather.10
  73.2 87.2 all-gather.12
  180.5 27.3 all-gather.10
  220.0 103.0 all-gather.12
  342.2 27.9 all-gather.10
  382.4 104.6 all-gather.12
  506.5 28.5 all-gather.10
  547.3 104.2 all-gather.12
  670.9 28.4 all-gather.10
  711.6 104.6 all-gather.12
  835.7 27.9 all-gather.10
  875.9 104.2 all-gather.12
  999.5 27.9 all-gather.10
  1039.7 105.5 all-gather.12
  1164.4 28.5 all-gather.10
  1205.2 105.1 all-gather.12
